TPU v7x, 512 devices: a whole 4x4x16 slice. The times are simulated.
512 devices in a mesh: occ: 64 (over y, z), vir: 8 (over x, core).
Axes of the slice: x: 4, y: 4, z: 16, core: 2. Of those that a mesh axis runs over, the one named last changes fastest.
Arguments:
- t2_tiles: bfloat16 [16384, 128, 128], P(('occ', 'vir')), may hold values from -6 to 6
- tile_owner: int32 [16384, 1], P(('occ', 'vir')), may hold values from 0 to 63; in each aligned block of 32 rows (0 to 31, 32 to 63, ...) at most 2 rows name the same one
- tile_block: int32 [16384], P(('occ', 'vir')), may hold values from 0 to 1
- tile_cd: int32 [16384], P(('occ', 'vir')), may hold values from 0 to 3
- ladder_ints: bfloat16 [4096, 2048], P('vir', 'occ'), may hold values from -0.75 to 0.75
- cycle_amps: bfloat16 [16384, 1024], P('occ', 'vir'), may hold values from -6 to 6
- cycle_ints: bfloat16 [1024, 2048], P('vir'), may hold values from -0.25 to 0.25
Outputs:
- residual: bfloat16 [16384, 2048], P('occ', 'vir')
Inputs may be any that keep to these rules, and one draw needn't show every extreme that they name: `tile_owner`: among the tiles of one device (aligned blocks of 32 tiles), no owner is named more than 2 times, a bound that some block reaches.
All inputs are finite; a program needn't handle non-finite values.
Results may differ from a plain program's by a relative error of at most 0.0048.
Values may be sent and summed in bfloat16 or wider, within the bound.
A program may use at most 64 MiB of HBM per device.

v0:
```python
import jax
import jax.numpy as jnp
from jax import lax
from jax.sharding import PartitionSpec as P

NY = 4


def body(t2_tiles, tile_owner, tile_block, tile_cd, ladder_ints, cycle_amps, cycle_ints):
    n_occ = lax.axis_size("occ")
    nz = n_occ // NY
    tile_count, tile_size = t2_tiles.shape[:2]
    pair_rows = cycle_amps.shape[0]
    blocks = pair_rows // tile_size
    cd_tiles = ladder_ints.shape[0] // tile_size
    combos = blocks * cd_tiles
    y_groups = [[y * nz + z for y in range(NY)] for z in range(nz)]
    z_groups = [[y * nz + z for z in range(nz)] for y in range(NY)]
    codes = tile_owner[:, 0] * combos + tile_block * cd_tiles + tile_cd
    got_tiles = lax.all_gather(
        t2_tiles.reshape(tile_count, tile_size * tile_size),
        "occ",
        axis=0,
        tiled=True,
        axis_index_groups=y_groups,
    )
    got_codes = lax.all_gather(codes, "occ", axis=0, tiled=True, axis_index_groups=y_groups)
    full_ladder = lax.all_gather(ladder_ints, "occ", axis=1, tiled=True)
    my_y = lax.axis_index("occ") // nz
    targets = my_y * (nz * combos) + jnp.arange(nz * combos, dtype=jnp.int32)
    select = (got_codes[:, None] == targets[None, :]).astype(jnp.bfloat16)
    summed = jnp.einsum("sc,sx->cx", select, got_tiles, preferred_element_type=jnp.float32)
    summed = lax.psum_scatter(
        summed.astype(jnp.bfloat16),
        "occ",
        scatter_dimension=0,
        tiled=True,
        axis_index_groups=z_groups,
    )
    amplitudes = (
        summed.reshape(blocks, cd_tiles, tile_size, tile_size)
        .transpose(0, 2, 1, 3)
        .reshape(pair_rows, cd_tiles * tile_size)
    )
    cycle_part = jnp.dot(cycle_amps, cycle_ints, preferred_element_type=jnp.float32)
    ladder = jnp.dot(amplitudes, full_ladder, preferred_element_type=jnp.float32)
    combined = ladder + cycle_part
    return lax.psum_scatter(combined, "vir", scatter_dimension=1, tiled=True).astype(jnp.bfloat16)


def solution(mesh):
    in_specs = (
        P(("occ", "vir"), None, None),
        P(("occ", "vir"), None),
        P(("occ", "vir")),
        P(("occ", "vir")),
        P("vir", "occ"),
        P("occ", "vir"),
        P("vir", None),
    )
    return jax.shard_map(
        body, mesh=mesh, in_specs=in_specs, out_specs=P("occ", "vir"), check_vma=False
    )
```

profile of v0, /device:TPU:8, one launch (start us, length us, event | category | flops | bytes accessed | tf_op | source)
XLA Modules:
  0.0 276.3 jit_solution(14078321033203667457)
XLA Ops:
  7.4 0.0 copy-start
  7.4 0.0 copy-start.2
  7.4 0.0 copy-start.4
  7.4 0.0 copy-start.3
  7.4 0.0 all-gather.3.cloned.1.call-start
  7.4 2.9 %copy.17 = bf16[4,8,128,128]{3,1,2,0:T(8,128)(2,1)} copy(bf16[4,8,128,128]{3,2,1,0:T(8,128)(2,1)} %bitcast.26) | data formatting | bytes 2097152
  10.3 0.0 all-gather.3.cloned.1.call-update
  10.4 0.0 reduce-scatter.3.cloned.1.call-start
  10.4 1.3 dynamic-slice
  12.4 0.0 copy-done.2
  12.4 0.0 copy-done.4
  12.4 0.0 copy-done.3
  12.4 0.1 fusion.6
  12.5 9.4 %all-reduce = s32[128]{0:T(128)S(1)} all-reduce(s32[128]{0:T(128)S(1)} %fusion.6), channel_id=1, replica_groups={{0,128,256,384},{8,136,264,392},{16,144,272,400},{24,152,280,408},{32,1..., use_global_device_ids=true, to_apply=%add | all-reduce | flops 128 | bytes 1024
  21.9 48.3 %all-gather.3.cloned.1.call-done = bf16[128,16384]{1,0:T(8,128)(2,1)} async-done(((bf16[32,16384]{1,0:T(8,128)(2,1)}), bf16[128,16384]{1,0:T(8,128)(2,1)}) %all-gather.3.cloned.1.call-update) | async-done | bytes 4194320 | tf_op jit(solution)/shard_map/all_gather | solution.py:20
  70.2 5.5 %convolution_convert_fusion = bf16[128,16384]{1,0:T(8,128)(2,1)} fusion(bf16[128,16384]{1,0:T(8,128)(2,1)} %all-gather.3.cloned.1.call-done, s32[128]{0:T(128)S(1)} %iota_add_fusion, s32[128]{0:T(128)S(1)} %all-reduce), kind=kOutput, calls=%fused_computation | convolution fusion | flops 538984448 | bytes 8389632 | tf_op jit(solution)/shard_map/sc,sx->cx/dot_general | solution.py:32
  75.7 0.0 copy-start.1
  75.7 0.0 reduce-scatter.3.cloned.1.call-update
  75.7 0.0 all-gather.5.cloned.1.call-start
  75.8 0.5 all-gather.5.cloned.1.call-update
  76.3 0.0 reduce-scatter.5.cloned.1.call-start
  76.4 0.0 copy-done
  76.4 0.2 copy-done.1
  76.5 0.4 fusion.7
  77.0 79.8 %reduce-scatter.3.cloned.1.call-done = bf16[8,16384]{1,0:T(8,128)(2,1)} async-done(((bf16[128,16384]{1,0:T(8,128)(2,1)}), bf16[8,16384]{1,0:T(8,128)(2,1)}) %reduce-scatter.3.cloned.1.call-update) | async-done | bytes 262160 | tf_op jit(solution)/shard_map/reduce_scatter | solution.py:33
  156.7 1.0 copy.10
  157.7 0.2 copy.8
  157.9 67.5 %all-gather.5.cloned.1.call-done = bf16[512,2048]{0,1:T(8,128)(2,1)} async-done(((bf16[512,32]{0,1:T(8,128)(2,1)}), bf16[512,2048]{0,1:T(8,128)(2,1)}) %all-gather.5.cloned.1.call-update) | async-done | bytes 2097168 | tf_op jit(solution)/shard_map/all_gather | solution.py:28
  225.4 3.7 %convolution_add_fusion = f32[256,2048]{1,0:T(8,128)} fusion(f32[256,2048]{1,0:T(8,128)S(1)} %fusion.7, bf16[512,2048]{0,1:T(8,128)(2,1)} %all-gather.5.cloned.1.call-done, bf16[32,8,4,128]{3,2,1,0:T(4,128)(2,1)S(1)} %bitcast.25), kind=kOutput, calls=%fused_computation.1 | convolution fusion | flops 537395200 | bytes 6553600 | tf_op jit(solution)/shard_map/dot_general | solution.py:46
  229.1 0.0 reduce-scatter.5.cloned.1.call-update
  229.1 38.2 %reduce-scatter.5.cloned.1.call-done = f32[256,256]{1,0:T(8,128)} async-done(((f32[256,2048]{1,0:T(8,128)}), f32[256,256]{1,0:T(8,128)}) %reduce-scatter.5.cloned.1.call-update) | async-done | bytes 262160 | tf_op jit(solution)/shard_map/reduce_scatter | solution.py:48
  267.3 1.6 convert_element_type.8
  (2 shorter events, 0.0 us)
Async XLA Ops:
  7.4 69.0 %copy-start = (bf16[128,2048]{1,0:T(8,128)(2,1)S(1)}, bf16[128,2048]{1,0:T(8,128)(2,1)}, u32[]{:S(2)}) copy-start(bf16[128,2048]{1,0:T(8,128)(2,1)} %param.13) | copy-start | bytes 1572868
  7.4 5.0 %copy-start.2 = (s32[32]{0:T(128)S(1)}, s32[32]{0:T(128)}, u32[]{:S(2)}) copy-start(s32[32]{0:T(128)} %param.10) | copy-start | bytes 388
  7.4 5.0 %copy-start.4 = (s32[32,1]{0,1:T(1,128)S(1)}, s32[32,1]{0,1:T(1,128)}, u32[]{:S(2)}) copy-start(s32[32,1]{0,1:T(1,128)} %param.8) | copy-start | bytes 388
  7.4 5.0 %copy-start.3 = (s32[32]{0:T(128)S(1)}, s32[32]{0:T(128)}, u32[]{:S(2)}) copy-start(s32[32]{0:T(128)} %param.9) | copy-start | bytes 388
  7.4 62.8 %all-gather.3.cloned.1.call-start = ((), (), s32[]{:S(2)}) async-start(), calls=%async_computation.2 | async-start | bytes 5242880 | tf_op jit(solution)/shard_map/all_gather | solution.py:20
  10.4 146.4 %reduce-scatter.3.cloned.1.call-start = ((), (), s32[]{:S(2)}) async-start(), calls=%async_computation.3 | async-start | bytes 4456448 | tf_op jit(solution)/shard_map/reduce_scatter | solution.py:33
  75.7 0.8 copy-start.1
  75.7 149.7 %all-gather.5.cloned.1.call-start = ((), (), s32[]{:S(2)}) async-start(), calls=%async_computation.4 | async-start | bytes 2129920 | tf_op jit(solution)/shard_map/all_gather | solution.py:28
  76.3 191.0 %reduce-scatter.5.cloned.1.call-start = ((), (), s32[]{:S(2)}) async-start(), calls=%async_computation.5 | async-start | bytes 2359296 | tf_op jit(solution)/shard_map/reduce_scatter | solution.py:48
Sparse Core Ops, SparseCore 0:
  10.5 59.6 all-gather.2
  75.8 80.8 reduce-scatter.2
Sparse Core Ops, SparseCore 1:
  79.1 146.2 all-gather.4
  229.2 38.0 reduce-scatter.4
where the time goes:
time: 277 us; the launch traced here: 276 us
  waiting for transfers between devices  234 us (84%)
  between operations  15.6 us (6%)
  matrix products  9.58 us (3%)
  blocking collectives  9.41 us (3%)
  local copies, waits for them, and re-layouts  5.58 us (2%)
    reduce_scatter x1, waiting for transfers between devices, body(): lax.psum_scatter(summed.astype(jnp.bfloat16), 'occ', scatter_dimension=0,...  79.8 us
    all_gather x1, waiting for transfers between devices, body(): full_ladder = lax.all_gather(ladder_ints, 'occ', axis=1, tiled=True)  67.5 us
    all_gather x1, waiting for transfers between devices, body(): lax.all_gather(t2_tiles.reshape(tile_count, tile_size * tile_size), 'occ'...  48.3 us
    reduce_scatter x1, waiting for transfers between devices, body(): lax.psum_scatter(combined, 'vir', scatter_dimension=1, tiled=True)  38.2 us
    unnamed x1, blocking collectives  9.41 us
  transfers between devices with their start and end apart: 4, of which 4 were waited for; matrix products, arithmetic and copies ran while one was open for 1% of the time, Pallas kernels for 0%

commit v1 on v0

--- a/solution.py
+++ b/solution.py
@@ -25,7 +25,9 @@
         axis_index_groups=y_groups,
     )
     got_codes = lax.all_gather(codes, "occ", axis=0, tiled=True, axis_index_groups=y_groups)
-    full_ladder = lax.all_gather(ladder_ints, "occ", axis=1, tiled=True)
+    full_ladder = jnp.concatenate(
+        lax.all_to_all(jnp.stack(lax.axis_size("occ") * [ladder_ints]), "occ", 0, 0), axis=1
+    )
     my_y = lax.axis_index("occ") // nz
     targets = my_y * (nz * combos) + jnp.arange(nz * combos, dtype=jnp.int32)
     select = (got_codes[:, None] == targets[None, :]).astype(jnp.bfloat16)

time: 277 us -> 290 us (1.047)
  starting transfers between devices: 0.16 us -> 15.7 us
  waiting for transfers between devices: 234 us -> 231 us
    all_gather x1 -> x0, waiting for transfers between devices: 67.5 us -> none  [body(): full_ladder = lax.all_gather(ladder_ints, 'occ', axis=1, tiled=True)]
    reduce_scatter x1, waiting for transfers between devices: 79.8 us -> 142 us  [body(): lax.psum_scatter(summed.astype(jnp.bfloat16), 'occ', scatter_dimension=0,...]
    all_to_all x0 -> x1, starting transfers between devices: none -> 15.6 us  [body(): lax.all_to_all(jnp.stack(lax.axis_size('occ') * [ladder_ints]), 'occ', 0, 0)]
    unnamed x14 -> x16, local copies, waits for them, and re-layouts: 5.37 us -> 5.93 us
  transfers between devices with their start and end apart: 4 -> 4, of which waited for: 4 -> 3; matrix products, arithmetic and copies ran while one was open for 1% -> 2% of each run, Pallas kernels for 0% -> 0%
where the time goes in v1:
time: 290 us
  waiting for transfers between devices  231 us (80%)
  starting transfers between devices  15.7 us (5%)
  between operations  13.9 us (5%)
  matrix products  10.9 us (4%)
  blocking collectives  9.41 us (3%)
  local copies, waits for them, and re-layouts  7.74 us (3%)
    reduce_scatter x1, waiting for transfers between devices, body(): lax.psum_scatter(summed.astype(jnp.bfloat16), 'occ', scatter_dimension=0,...  142 us
    all_gather x1, waiting for transfers between devices, body(): lax.all_gather(t2_tiles.reshape(tile_count, tile_size * tile_size), 'occ'...  48.3 us
    reduce_scatter x1, waiting for transfers between devices, body(): lax.psum_scatter(combined, 'vir', scatter_dimension=1, tiled=True)  40.6 us
    all_to_all x1, starting transfers between devices, body(): lax.all_to_all(jnp.stack(lax.axis_size('occ') * [ladder_ints]), 'occ', 0, 0)  15.6 us
    unnamed x1, blocking collectives  9.41 us
    unnamed x16, local copies, waits for them, and re-layouts  5.93 us
  transfers between devices with their start and end apart: 4, of which 3 were waited for; matrix products, arithmetic and copies ran while one was open for 2% of the time, Pallas kernels for 0%

profile of v1, /device:TPU:8, one launch (start us, length us, event | category | flops | bytes accessed | tf_op | source)
XLA Modules:
  0.0 289.9 jit_solution(11249092823229394430)
XLA Ops:
  6.5 0.0 copy-start
  6.5 0.0 copy-start.3
  6.5 0.0 copy-start.4
  6.5 0.0 copy-start.5
  6.5 0.0 all-gather.2.cloned.1.call-start
  6.6 2.9 %copy.18 = bf16[4,8,128,128]{3,1,2,0:T(8,128)(2,1)} copy(bf16[4,8,128,128]{3,2,1,0:T(8,128)(2,1)} %bitcast.30) | data formatting | bytes 2097152
  9.5 0.0 all-gather.2.cloned.1.call-update
  9.5 0.0 reduce-scatter.3.cloned.1.call-start
  9.6 1.3 dynamic-slice
  11.5 0.0 copy-done.3
  11.5 0.0 copy-done.4
  11.5 0.0 copy-done.5
  11.6 0.1 fusion.6
  11.7 9.4 %all-reduce = s32[128]{0:T(128)S(1)} all-reduce(s32[128]{0:T(128)S(1)} %fusion.6), channel_id=1, replica_groups={{0,128,256,384},{8,136,264,392},{16,144,272,400},{24,152,280,408},{32,1..., use_global_device_ids=true, to_apply=%add | all-reduce | flops 128 | bytes 1024
  21.1 48.3 %all-gather.2.cloned.1.call-done = bf16[128,16384]{1,0:T(8,128)(2,1)} async-done(((bf16[32,16384]{1,0:T(8,128)(2,1)}), bf16[128,16384]{1,0:T(8,128)(2,1)}) %all-gather.2.cloned.1.call-update) | async-done | bytes 4194320 | tf_op jit(solution)/shard_map/all_gather | solution.py:20
  69.4 5.5 %convolution_convert_fusion = bf16[128,16384]{1,0:T(8,128)(2,1)} fusion(bf16[128,16384]{1,0:T(8,128)(2,1)} %all-gather.2.cloned.1.call-done, s32[128]{0:T(128)S(1)} %iota_add_fusion, s32[128]{0:T(128)S(1)} %all-reduce), kind=kOutput, calls=%fused_computation | convolution fusion | flops 538984448 | bytes 8389632 | tf_op jit(solution)/shard_map/sc,sx->cx/dot_general | solution.py:34
  74.9 0.0 copy-start.2
  74.9 0.0 reduce-scatter.3.cloned.1.call-update
  74.9 0.7 copy-done.2
  75.6 1.6 stack.2
  77.2 0.0 copy-start.1
  77.2 15.6 %all-to-all-start = ((bf16[64,512,32]{1,2,0:T(8,128)(2,1)}), bf16[64,512,32]{1,2,0:T(8,128)(2,1)S(1)}, u32[]{:S(2)}, u32[]{:S(2)}) async-start(bf16[64,512,32]{1,2,0:T(8,128)(2,1)} %stack.2), calls=%async_computation.1 | async-start | bytes 4194304 | tf_op jit(solution)/shard_map/all_to_all | solution.py:29
  92.8 0.0 reduce-scatter.5.cloned.1.call-start
  92.9 0.0 copy-done
  92.9 0.0 copy-done.1
  92.9 1.7 fusion.7
  94.6 141.6 %reduce-scatter.3.cloned.1.call-done = bf16[8,16384]{1,0:T(8,128)(2,1)} async-done(((bf16[128,16384]{1,0:T(8,128)(2,1)}), bf16[8,16384]{1,0:T(8,128)(2,1)}) %reduce-scatter.3.cloned.1.call-update) | async-done | bytes 262160 | tf_op jit(solution)/shard_map/reduce_scatter | solution.py:35
  236.3 1.0 copy.11
  237.3 0.2 copy.9
  237.5 0.0 all-to-all-done
  237.5 3.7 %convolution_add_fusion = f32[256,2048]{1,0:T(8,128)} fusion(f32[256,2048]{1,0:T(8,128)} %fusion.7, bf16[512,2048]{0,1:T(8,128)(2,1)S(1)} %bitcast.27, bf16[32,8,4,128]{3,2,1,0:T(4,128)(2,1)S(1)} %bitcast.29), kind=kOutput, calls=%fused_computation.1 | convolution fusion | flops 537395200 | bytes 6553600 | tf_op jit(solution)/shard_map/dot_general | solution.py:48
  241.1 0.0 reduce-scatter.5.cloned.1.call-update
  241.2 40.6 %reduce-scatter.5.cloned.1.call-done = f32[256,256]{1,0:T(8,128)} async-done(((f32[256,2048]{1,0:T(8,128)}), f32[256,256]{1,0:T(8,128)}) %reduce-scatter.5.cloned.1.call-update) | async-done | bytes 262160 | tf_op jit(solution)/shard_map/reduce_scatter | solution.py:50
  281.8 1.6 convert_element_type.8
  (2 shorter events, 0.0 us)
Async XLA Ops:
  6.5 86.3 %copy-start = (bf16[128,2048]{1,0:T(8,128)(2,1)S(1)}, bf16[128,2048]{1,0:T(8,128)(2,1)}, u32[]{:S(2)}) copy-start(bf16[128,2048]{1,0:T(8,128)(2,1)} %param.13) | copy-start | bytes 1572868
  6.5 5.0 %copy-start.3 = (s32[32]{0:T(128)S(1)}, s32[32]{0:T(128)}, u32[]{:S(2)}) copy-start(s32[32]{0:T(128)} %param.10) | copy-start | bytes 388
  6.5 5.0 %copy-start.4 = (s32[32]{0:T(128)S(1)}, s32[32]{0:T(128)}, u32[]{:S(2)}) copy-start(s32[32]{0:T(128)} %param.9) | copy-start | bytes 388
  6.5 5.0 %copy-start.5 = (s32[32,1]{0,1:T(1,128)S(1)}, s32[32,1]{0,1:T(1,128)}, u32[]{:S(2)}) copy-start(s32[32,1]{0,1:T(1,128)} %param.8) | copy-start | bytes 388
  6.5 62.8 %all-gather.2.cloned.1.call-start = ((), (), s32[]{:S(2)}) async-start(), calls=%async_computation.3 | async-start | bytes 5242880 | tf_op jit(solution)/shard_map/all_gather | solution.py:20
  9.5 226.7 %reduce-scatter.3.cloned.1.call-start = ((), (), s32[]{:S(2)}) async-start(), calls=%async_computation.4 | async-start | bytes 4456448 | tf_op jit(solution)/shard_map/reduce_scatter | solution.py:35
  74.9 0.8 copy-start.2
  77.2 15.6 %copy-start.1 = (bf16[256,128]{1,0:T(8,128)(2,1)S(1)}, bf16[256,128]{1,0:T(8,128)(2,1)}, u32[]{:S(2)}) copy-start(bf16[256,128]{1,0:T(8,128)(2,1)} %param.12) | copy-start | bytes 196612
  77.2 160.2 %all-to-all-start = ((bf16[64,512,32]{1,2,0:T(8,128)(2,1)}), bf16[64,512,32]{1,2,0:T(8,128)(2,1)S(1)}, u32[]{:S(2)}, u32[]{:S(2)}) async-start(bf16[64,512,32]{1,2,0:T(8,128)(2,1)} %stack.2), calls=%async_computation.1 | async-start | bytes 4194304 | tf_op jit(solution)/shard_map/all_to_all | solution.py:29
  92.8 189.0 %reduce-scatter.5.cloned.1.call-start = ((), (), s32[]{:S(2)}) async-start(), calls=%async_computation.5 | async-start | bytes 2359296 | tf_op jit(solution)/shard_map/reduce_scatter | solution.py:50
Sparse Core Ops, SparseCore 0:
  9.7 59.6 all-gather.1
  75.0 161.2 reduce-scatter.2
  241.3 40.4 reduce-scatter.4
